TPU v7x, 32 devices: a whole 2x2x4 slice. The times are simulated.
32 devices in a mesh: row: 4 (over y, core), col: 8 (over z, x).
Axes of the slice: x: 2, y: 2, z: 4, core: 2. Of those that a mesh axis runs over, the one named last changes fastest.
Arguments:
- stored: float32 [40, 4, 128, 20, 8, 128], P(None, 'row', None, None, 'col'), may hold values from -1 to 13
- rhs: float32 [20, 8, 128, 128], P(None, 'col'), may hold values from -60 to 60
Outputs:
- solution: float32 [20, 8, 128, 128], P(None, 'col')
- residual: float32 [20, 8, 128, 128], P(None, 'col')
All inputs are finite; a program needn't handle non-finite values.
Results may differ from a plain program's by a relative error of at most 0.0003.
Values sent between devices are 32-bit elements; how exact they have to be, the bound alone decides.
No kernel may reach another device: no remote copies, remote signals or barrier semaphores. Data moves between devices by JAX's collectives and lax.ppermute only.
A program may use at most 192 MiB of HBM per device.

v0:
```python
import jax
import jax.numpy as jnp
from jax import lax
from jax.sharding import PartitionSpec as P

ITERS = 2
HIGHEST = lax.Precision.HIGHEST


def partner_2(value, axis, distance):
    mask = 2**distance
    pairs = [(source, source ^ mask) for source in range(lax.axis_size(axis))]
    return lax.ppermute(value, axis, pairs)


def spread(value, axis, source):
    kept = jnp.where(lax.axis_index(axis) == source, value, 0).astype(value.dtype)
    return lax.psum(kept, axis)


def gram_local(left_side, right_side):
    columns_n = left_side.shape[-1]
    return jnp.einsum(
        "nk,nl->kl",
        left_side.reshape(-1, columns_n),
        right_side.reshape(-1, columns_n),
        precision=HIGHEST,
        preferred_element_type=jnp.float32,
    )


def mix_right(vectors, matrix):
    columns_n = vectors.shape[-1]
    return jnp.dot(
        vectors.reshape(-1, columns_n),
        matrix,
        precision=HIGHEST,
        preferred_element_type=jnp.float32,
    ).reshape(vectors.shape)


def solve_spd(matrix, target):
    factor = jnp.linalg.cholesky(matrix)
    return jax.scipy.linalg.cho_solve((factor, True), target)


def to_rowset(column_set, row_index, col_index):
    low_bits = lax.axis_size("row").bit_length() - 1
    high_bits = lax.axis_size("col").bit_length() - 1
    current = column_set
    for bit_pos in range(low_bits):
        partner = partner_2(current, "col", bit_pos)
        differs = col_index >> bit_pos & 1 != row_index >> bit_pos & 1
        current = jnp.where(differs, partner, current)
    joined = current[:, None]
    for bit_pos in range(low_bits, high_bits):
        partner = partner_2(joined, "col", bit_pos)
        lower_half = col_index >> bit_pos & 1 == 0
        joined = jnp.where(
            lower_half,
            jnp.concatenate([joined, partner], axis=1),
            jnp.concatenate([partner, joined], axis=1),
        )
    return joined.reshape((-1,) + column_set.shape[1:])


def to_colset(row_set, col_index):
    rows_n = lax.axis_size("row")
    groups = lax.axis_size("col") // rows_n
    shape_in = row_set.shape
    regrouped = row_set.reshape(shape_in[:-3] + (shape_in[-3] // groups, groups) + shape_in[-2:])
    selected = lax.dynamic_index_in_dim(
        regrouped, col_index // rows_n, regrouped.ndim - 3, keepdims=False
    )
    return spread(selected, "row", col_index % rows_n)


def local_products(lower_part, column_set, row_set):
    columns_n = column_set.shape[-1]
    by_rows = jnp.dot(
        lower_part,
        column_set.reshape(-1, columns_n),
        precision=HIGHEST,
        preferred_element_type=jnp.float32,
    )
    by_columns = jnp.einsum(
        "nm,nk->mk",
        lower_part,
        row_set.reshape(-1, columns_n),
        precision=HIGHEST,
        preferred_element_type=jnp.float32,
    )
    return (by_rows, by_columns)


def columns_whole(by_columns, shape_out):
    return lax.psum(by_columns, "row").reshape(shape_out)


def rows_whole(by_rows, shape_out):
    return lax.psum(by_rows, "col").reshape(shape_out)


def per_device(stored, rhs):
    row_index = lax.axis_index("row")
    col_index = lax.axis_index("col")
    rows_n = lax.axis_size("row")
    cols_n = lax.axis_size("col")
    row_blocks = stored.shape[0]
    block_size = stored.shape[2]
    col_blocks = stored.shape[3]
    columns_n = rhs.shape[-1]
    block_rows = jnp.arange(row_blocks, dtype=jnp.int32) * rows_n + row_index
    block_cols = jnp.arange(col_blocks, dtype=jnp.int32) * cols_n + col_index
    weight = jnp.where(
        block_rows[:, None] > block_cols[None, :],
        1.0,
        jnp.where(block_rows[:, None] == block_cols[None, :], 0.5, 0.0),
    ).astype(jnp.float32)
    lower_part = (
        stored.reshape(row_blocks, block_size, col_blocks, block_size) * weight[:, None, :, None]
    ).reshape(row_blocks * block_size, col_blocks * block_size)
    start_set = rhs.reshape(col_blocks, block_size, columns_n)

    def reduce_grams(stacked):
        return lax.psum(stacked, "col")

    solution = jnp.zeros_like(start_set)
    residual = start_set
    direction = start_set
    gram_now = reduce_grams(gram_local(residual, residual)[None])[0]
    for iteration in range(ITERS):
        row_set = to_rowset(direction, row_index, col_index)
        by_rows, by_columns = local_products(lower_part, direction, row_set)
        column_part = columns_whole(by_columns, direction.shape)
        row_piece = to_colset(rows_whole(by_rows, row_set.shape), col_index)
        applied = column_part + row_piece
        last_turn = iteration + 1 == ITERS
        gram_sums = reduce_grams(gram_local(direction, applied)[None])
        curvature = gram_sums[0]
        step_size = solve_spd(curvature, gram_now)
        solution = solution + mix_right(direction, step_size)
        residual = residual - mix_right(applied, step_size)
        if not last_turn:
            gram_next = reduce_grams(gram_local(residual, residual)[None])[0]
            mix_factor = solve_spd(gram_now, gram_next)
            direction = residual + mix_right(direction, mix_factor)
            gram_now = gram_next
    final_pair = (solution, residual)
    return (final_pair[0].reshape(rhs.shape), final_pair[1].reshape(rhs.shape))


def solution(mesh):
    placed = (P(None, "row", None, None, "col", None), P(None, "col", None, None))
    return jax.shard_map(
        per_device,
        mesh=mesh,
        in_specs=placed,
        out_specs=(P(None, "col", None, None), P(None, "col", None, None)),
        check_vma=False,
    )
```

profile of v0, /device:TPU:0, one launch (start us, length us, event | category | flops | bytes accessed | tf_op | source)
XLA Modules:
  0.0 1001.4 jit_solution(6003752556516424082)
XLA Ops:
  7.2 3.0 collective-permute-start
  10.3 28.9 %collective-permute-done = f32[20,128,128]{2,1,0:T(8,128)S(1)} collective-permute-done((f32[20,128,128]{2,1,0:T(8,128)}, f32[20,128,128]{2,1,0:T(8,128)S(1)}, u32[]{:S(2)}, u32[]{:S(2)}) %collective-permute-start) | collective-permute-done | bytes 1310752 | tf_op jit(solution)/shard_map/ppermute | solution.py:13
  42.6 163.2 %multiply_reduce_fusion = f32[40,128,20,128]{3,2,1,0:T(8,128)} fusion(f32[40,1,128,20,1,128]{5,4,3,2,1,0:T(1,128)} %param.5, f32[40,20]{1,0:T(8,128)S(1)} %select_select_fusion.3), kind=kLoop, calls=%fused_computation.8 | loop fusion | flops 13107200 | bytes 104860800 | tf_op jit(solution)/shard_map/mul | solution.py:121
  207.0 2.6 collective-permute-start.2
  209.6 52.8 %fusion.4 = f32[5120,128]{1,0:T(8,128)S(1)} fusion(f32[2560,128]{1,0:T(8,128)S(1)} %bitcast.123, f32[640,8,20,128]{3,2,1,0:T(8,128)} %bitcast.118), kind=kOutput, calls=%fused_computation.4 | convolution fusion | flops 20132659200 | bytes 56360960 | tf_op jit(solution)/shard_map/dot_general | solution.py:80
  267.8 106.5 %fusion.6 = f32[2560,128]{1,0:T(8,128)S(1)} fusion(f32[5120,128]{1,0:T(8,128)S(1)} %bitcast.129, f32[640,8,20,128]{3,2,1,0:T(8,128)} %bitcast.119), kind=kOutput, calls=%fused_computation.6 | convolution fusion | flops 20132659200 | bytes 56360960 | tf_op jit(solution)/shard_map/nm,nk->mk/dot_general | solution.py:86
  374.4 5.6 all-reduce.9.cloned.1.call-done
  382.6 2.9 convolution_bitcast_fusion.5
  385.4 35.7 %all-reduce.17.cloned.1.call-done = f32[20,128,128]{2,1,0:T(8,128)} async-done(((f32[20,128,128]{2,1,0:T(8,128)}), f32[20,128,128]{2,1,0:T(8,128)}) %all-reduce.17.cloned.1.call-update) | async-done | bytes 1310736 | tf_op jit(solution)/shard_map/psum | solution.py:97
  421.1 4.2 convolution_bitcast_fusion.6
  425.3 70.8 %all-reduce.21.cloned.1.call-done = (f32[128,128]{0,1:T(8,128)}, f32[128,128]{0,1:T(8,128)}) async-done(((f32[128,128]{0,1:T(8,128)}, f32[128,128]{0,1:T(8,128)}), (f32[128,128]{0,1:T(8,128)}, f32[128,128]{0,1:T(8,128)})) %all-reduce.21.cloned.1.call-update) | async-done | bytes 131088 | tf_op jit(solution)/shard_map/psum | solution.py:126
  498.9 11.7 %cholesky.70 = f32[128,128]{1,0:T(8,128)S(1)} custom-call(f32[128,128]{1,0:T(8,128)S(1)} %get-tuple-element.10), custom_call_target="Cholesky" | custom-call | tf_op jit(solution)/shard_map/jit(cholesky)/cholesky | solution.py:43
  511.3 11.7 %cholesky.59 = f32[128,128]{1,0:T(8,128)S(1)} custom-call(f32[128,128]{1,0:T(8,128)S(1)} %get-tuple-element.11), custom_call_target="Cholesky" | custom-call | tf_op jit(solution)/shard_map/jit(cholesky)/cholesky | solution.py:43
  524.3 9.8 custom-call.9
  538.0 3.3 convolution_bitcast_fusion.4
  542.0 9.8 custom-call.10
  551.8 58.1 %all-reduce.11.cloned.1.call-done = f32[128,128]{1,0:T(8,128)} async-done(((f32[128,128]{1,0:T(8,128)}), f32[128,128]{1,0:T(8,128)}) %all-reduce.11.cloned.1.call-update) | async-done | bytes 65552 | tf_op jit(solution)/shard_map/psum | solution.py:126
  613.6 2.8 copy.25
  619.3 27.2 %collective-permute-done.3 = f32[20,128,128]{2,1,0:T(8,128)S(1)} collective-permute-done((f32[20,128,128]{2,1,0:T(8,128)S(1)}, f32[20,128,128]{2,1,0:T(8,128)S(1)}, u32[]{:S(2)}, u32[]{:S(2)}) %collective-permute-start.3) | collective-permute-done | bytes 1310752 | tf_op jit(solution)/shard_map/ppermute | solution.py:13
  648.3 26.3 %collective-permute-done.4 = f32[20,128,128]{2,1,0:T(8,128)S(1)} collective-permute-done((f32[20,128,128]{2,1,0:T(8,128)S(1)}, f32[20,128,128]{2,1,0:T(8,128)S(1)}, u32[]{:S(2)}, u32[]{:S(2)}) %collective-permute-start.4) | collective-permute-done | bytes 1310752 | tf_op jit(solution)/shard_map/ppermute | solution.py:13
  677.7 52.8 %fusion = f32[5120,128]{1,0:T(8,128)S(1)} fusion(f32[2560,128]{1,0:T(8,128)S(1)} %bitcast.127, f32[640,8,20,128]{3,2,1,0:T(8,128)} %bitcast.120), kind=kOutput, calls=%fused_computation | convolution fusion | flops 20132659200 | bytes 56360960 | tf_op jit(solution)/shard_map/dot_general | solution.py:80
  732.3 3.0 maximum_select_fusion.1
  735.6 95.9 %fusion.2 = f32[2560,128]{1,0:T(8,128)} fusion(f32[5120,128]{1,0:T(8,128)S(1)} %bitcast.128, f32[640,8,20,128]{3,2,1,0:T(8,128)} %bitcast.121), kind=kOutput, calls=%fused_computation.2 | convolution fusion | flops 20132659200 | bytes 56360960 | tf_op jit(solution)/shard_map/nm,nk->mk/dot_general | solution.py:86
  831.4 16.4 %all-reduce.13.cloned.1.call-done = f32[20,2,128,128]{3,2,0,1:T(8,128)} async-done(((f32[20,2,128,128]{3,2,0,1:T(8,128)}), f32[20,2,128,128]{3,2,0,1:T(8,128)}) %all-reduce.13.cloned.1.call-update) | async-done | bytes 2621456 | tf_op jit(solution)/shard_map/psum | solution.py:101
  847.8 2.9 bitcast_add_fusion
  850.8 38.2 %all-reduce.19.cloned.1.call-done = f32[20,128,128]{2,1,0:T(8,128)} async-done(((f32[20,128,128]{2,1,0:T(8,128)}), f32[20,128,128]{2,1,0:T(8,128)}) %all-reduce.19.cloned.1.call-update) | async-done | bytes 1310736 | tf_op jit(solution)/shard_map/psum | solution.py:97
  889.1 4.6 convolution_bitcast_fusion.3
  896.0 2.9 copy.22
  898.9 64.2 %all-reduce.15.cloned.1.call-done = f32[128,128]{0,1:T(8,128)} async-done(((f32[128,128]{0,1:T(8,128)}), f32[128,128]{0,1:T(8,128)}) %all-reduce.15.cloned.1.call-update) | async-done | bytes 65552 | tf_op jit(solution)/shard_map/psum | solution.py:126
  964.9 11.7 %cholesky.81 = f32[128,128]{1,0:T(8,128)S(1)} custom-call(f32[128,128]{1,0:T(8,128)S(1)} %fusion.20), custom_call_target="Cholesky" | custom-call | tf_op jit(solution)/shard_map/jit(cholesky)/cholesky | solution.py:43
  977.9 9.8 custom-call.11
  988.3 3.7 fusion.12
  (69 shorter events, 43.8 us)
Async XLA Ops:
  7.2 372.8 %all-reduce.9.cloned.1.call-start = ((), (), s32[]{:S(2)}) async-start(), calls=%async_computation | async-start | bytes 5242880 | tf_op jit(solution)/shard_map/psum | solution.py:101
  7.2 32.0 %collective-permute-start = (f32[20,128,128]{2,1,0:T(8,128)}, f32[20,128,128]{2,1,0:T(8,128)S(1)}, u32[]{:S(2)}, u32[]{:S(2)}) collective-permute-start(f32[20,128,128]{2,1,0:T(8,128)} %bitcast.122), channel_id=1, source_target_pairs={{0,1},{1,0},{2,3},{3,2},{4,5},{5,4},{6,7},{7,6},{8,9},{9,8},{10,11... | collective-permute-start | bytes 3932168 | tf_op jit(solution)/shard_map/ppermute | solution.py:13
  40.7 165.1 %collective-permute-start.1 = (f32[20,128,128]{2,1,0:T(8,128)S(1)}, f32[20,128,128]{2,1,0:T(8,128)}, u32[]{:S(2)}, u32[]{:S(2)}) collective-permute-start(f32[20,128,128]{2,1,0:T(8,128)S(1)} %broadcast_select_fusion.1), channel_id=1, source_target_pairs={{0,2},{1,3},{2,0},{3,1},{4,6},{5,7},{6,4},{7,5},{8,10},{9,11},{10,... | collective-permute-start | bytes 3932168 | tf_op jit(solution)/shard_map/ppermute | solution.py:13
  205.8 3.8 copy-start
  207.0 58.6 %collective-permute-start.2 = (f32[20,1,128,128]{3,2,0,1:T(8,128)}, f32[20,1,128,128]{3,2,0,1:T(8,128)S(1)}, u32[]{:S(2)}, u32[]{:S(2)}) collective-permute-start(f32[20,1,128,128]{3,2,0,1:T(8,128)} %select_bitcast_fusion.1), channel_id=1, source_target_pairs={{0,4},{1,5},{2,6},{3,7},{4,0},{5,1},{6,2},{7,3},{8,12},{9,13},{10,... | collective-permute-start | bytes 3932168 | tf_op jit(solution)/shard_map/ppermute | solution.py:13
  264.2 156.9 %all-reduce.17.cloned.1.call-start = ((), (), s32[]{:S(2)}) async-start(), calls=%async_computation.4 | async-start | bytes 2621440 | tf_op jit(solution)/shard_map/psum | solution.py:97
  382.5 113.6 %all-reduce.21.cloned.1.call-start = ((), (), s32[]{:S(2)}) async-start(), calls=%async_computation.6 | async-start | bytes 262144 | tf_op jit(solution)/shard_map/psum | solution.py:126
  425.3 184.6 %all-reduce.11.cloned.1.call-start = ((), (), s32[]{:S(2)}) async-start(), calls=%async_computation.1 | async-start | bytes 131072 | tf_op jit(solution)/shard_map/psum | solution.py:126
  541.3 306.5 %all-reduce.13.cloned.1.call-start = ((), (), s32[]{:S(2)}) async-start(), calls=%async_computation.2 | async-start | bytes 5242880 | tf_op jit(solution)/shard_map/psum | solution.py:101
  617.8 59.9 %copy-start.1 = (f32[20,128,128]{2,1,0:T(8,128)}, f32[20,128,128]{2,1,0:T(8,128)S(1)}, u32[]{:S(2)}) copy-start(f32[20,128,128]{2,1,0:T(8,128)S(1)} %add.81) | copy-start | bytes 3932164
  617.8 28.7 %collective-permute-start.3 = (f32[20,128,128]{2,1,0:T(8,128)S(1)}, f32[20,128,128]{2,1,0:T(8,128)S(1)}, u32[]{:S(2)}, u32[]{:S(2)}) collective-permute-start(f32[20,128,128]{2,1,0:T(8,128)S(1)} %add.81), channel_id=1, source_target_pairs={{0,1},{1,0},{2,3},{3,2},{4,5},{5,4},{6,7},{7,6},{8,9},{9,8},{10,11... | collective-permute-start | bytes 3932168 | tf_op jit(solution)/shard_map/ppermute | solution.py:13
  646.7 27.9 %collective-permute-start.4 = (f32[20,128,128]{2,1,0:T(8,128)S(1)}, f32[20,128,128]{2,1,0:T(8,128)S(1)}, u32[]{:S(2)}, u32[]{:S(2)}) collective-permute-start(f32[20,128,128]{2,1,0:T(8,128)S(1)} %broadcast_select_fusion), channel_id=1, source_target_pairs={{0,2},{1,3},{2,0},{3,1},{4,6},{5,7},{6,4},{7,5},{8,10},{9,11},{10,... | collective-permute-start | bytes 3932168 | tf_op jit(solution)/shard_map/ppermute | solution.py:13
  675.8 56.5 %collective-permute-start.5 = (f32[20,1,128,128]{3,2,0,1:T(8,128)}, f32[20,1,128,128]{3,2,0,1:T(8,128)}, u32[]{:S(2)}, u32[]{:S(2)}) collective-permute-start(f32[20,1,128,128]{3,2,0,1:T(8,128)} %select_bitcast_fusion), channel_id=1, source_target_pairs={{0,4},{1,5},{2,6},{3,7},{4,0},{5,1},{6,2},{7,3},{8,12},{9,13},{10,... | collective-permute-start | bytes 3932168 | tf_op jit(solution)/shard_map/ppermute | solution.py:13
  732.3 156.8 %all-reduce.19.cloned.1.call-start = ((), (), s32[]{:S(2)}) async-start(), calls=%async_computation.5 | async-start | bytes 2621440 | tf_op jit(solution)/shard_map/psum | solution.py:97
  850.8 112.3 %all-reduce.15.cloned.1.call-start = ((), (), s32[]{:S(2)}) async-start(), calls=%async_computation.3 | async-start | bytes 131072 | tf_op jit(solution)/shard_map/psum | solution.py:126
  896.0 91.7 %copy-start.4 = (f32[128,128]{1,0:T(8,128)S(1)}, f32[128,128]{1,0:T(8,128)}, u32[]{:S(2)}) copy-start(f32[128,128]{1,0:T(8,128)} %all-reduce.11.cloned.1.call-done) | copy-start | bytes 196612
  896.0 92.3 %copy-start.2 = (f32[20,128,128]{2,1,0:T(8,128)S(1)}, f32[20,128,128]{2,1,0:T(8,128)}, u32[]{:S(2)}) copy-start(f32[20,128,128]{2,1,0:T(8,128)} %copy-done.1) | copy-start | bytes 3932164
  988.3 3.7 copy-start.3
Sparse Core Ops, SparseCore 0:
  264.3 115.6 all-reduce.8
  382.9 38.1 all-reduce.16
  425.4 70.6 all-reduce.20
  541.4 68.4 all-reduce.10
  732.4 115.3 all-reduce.12
  850.9 38.1 all-reduce.18
  893.8 69.2 all-reduce.14
where the time goes:
time: 1010 us; the launch traced here: 1000 us
  waiting for transfers between devices  373 us (37%)
  matrix products  339 us (34%)
  other arithmetic  250 us (25%)
  between operations  14.8 us (1%)
  starting transfers between devices  12.9 us (1%)
  local copies, waits for them, and re-layouts  12.2 us (1%)
    dot_general x2, matrix products, local_products(): jnp.einsum('nm,nk->mk', lower_part, row_set.reshape(-1, columns_n), preci...  202 us
    psum x3, waiting for transfers between devices, reduce_grams(): return lax.psum(stacked, 'col')  193 us
    mul x1, other arithmetic, per_device(): stored.reshape(row_blocks, block_size, col_blocks, block_size)  163 us
    dot_general x2, matrix products, local_products(): jnp.dot(lower_part, column_set.reshape(-1, columns_n), precision=HIGHEST,...  106 us
    ppermute x6, waiting for transfers between devices, partner_2(): return lax.ppermute(value, axis, pairs)  83.8 us
    psum x2, waiting for transfers between devices, columns_whole(): return lax.psum(by_columns, 'row').reshape(shape_out)  73.9 us
    another operation x9, other arithmetic, solve_spd(): factor = jnp.linalg.cholesky(matrix)  37.2 us
    another operation x6, other arithmetic, solve_spd(): return jax.scipy.linalg.cho_solve((factor, True), target)  31.4 us
  transfers between devices with their start and end apart: 13, of which 11 were waited for; matrix products, arithmetic and copies ran while one was open for 50% of the time, Pallas kernels for 0%

commit v1 on v0

--- a/solution.py
+++ b/solution.py
@@ -123,7 +123,11 @@
     start_set = rhs.reshape(col_blocks, block_size, columns_n)
 
     def reduce_grams(stacked):
-        return lax.psum(stacked, "col")
+
+        def proceed_the_sheets(unit, mesh_dim):
+            return jnp.sum(jax.lax.all_gather(unit, mesh_dim), 0)
+
+        return proceed_the_sheets(stacked, "col")
 
     solution = jnp.zeros_like(start_set)
     residual = start_set

time: 1010 us -> 881 us (0.87)
  waiting for transfers between devices: 373 us -> 139 us
  blocking collectives: 0 us -> 128 us
  matrix products: 339 us -> 322 us
    psum x3 -> x0, waiting for transfers between devices: 193 us -> none  [reduce_grams(): return lax.psum(stacked, 'col')]
    all_gather x0 -> x4, blocking collectives: none -> 128 us  [proceed_the_sheets(): return jnp.sum(jax.lax.all_gather(unit, mesh_dim), 0)]
    psum x2, waiting for transfers between devices: 73.9 us -> 49.4 us  [columns_whole(): return lax.psum(by_columns, 'row').reshape(shape_out)]
    dot_general x2, matrix products: 202 us -> 190 us  [local_products(): jnp.einsum('nm,nk->mk', lower_part, row_set.reshape(-1, columns_n), preci...]
    ppermute x6, waiting for transfers between devices: 83.8 us -> 72.7 us  [partner_2(): return lax.ppermute(value, axis, pairs)]
  transfers between devices with their start and end apart: 13 -> 10, of which waited for: 11 -> 6; matrix products, arithmetic and copies ran while one was open for 50% -> 57% of each run, Pallas kernels for 0% -> 0%
where the time goes in v1:
time: 881 us; the launch traced here: 872 us
  matrix products  322 us (37%)
  other arithmetic  248 us (28%)
  waiting for transfers between devices  139 us (16%)
  blocking collectives  128 us (15%)
  between operations  14.5 us (2%)
  starting transfers between devices  10.6 us (1%)
  local copies, waits for them, and re-layouts  9.81 us (1%)
    dot_general x2, matrix products, local_products(): jnp.einsum('nm,nk->mk', lower_part, row_set.reshape(-1, columns_n), preci...  190 us
    mul x1, other arithmetic, per_device(): stored.reshape(row_blocks, block_size, col_blocks, block_size)  163 us
    all_gather x4, blocking collectives, proceed_the_sheets(): return jnp.sum(jax.lax.all_gather(unit, mesh_dim), 0)  128 us
    dot_general x2, matrix products, local_products(): jnp.dot(lower_part, column_set.reshape(-1, columns_n), precision=HIGHEST,...  106 us
    ppermute x6, waiting for transfers between devices, partner_2(): return lax.ppermute(value, axis, pairs)  72.7 us
    psum x2, waiting for transfers between devices, columns_whole(): return lax.psum(by_columns, 'row').reshape(shape_out)  49.4 us
    another operation x9, other arithmetic, solve_spd(): factor = jnp.linalg.cholesky(matrix)  37.2 us
    another operation x6, other arithmetic, solve_spd(): return jax.scipy.linalg.cho_solve((factor, True), target)  31.4 us
  transfers between devices with their start and end apart: 10, of which 6 were waited for; matrix products, arithmetic and copies ran while one was open for 57% of the time, Pallas kernels for 0%

profile of v1, /device:TPU:0, one launch (start us, length us, event | category | flops | bytes accessed | tf_op | source)
XLA Modules:
  0.0 872.2 jit_solution(5936378109173707121)
XLA Ops:
  7.2 3.0 collective-permute-start
  10.3 28.9 %collective-permute-done = f32[20,128,128]{2,1,0:T(8,128)S(1)} collective-permute-done((f32[20,128,128]{2,1,0:T(8,128)}, f32[20,128,128]{2,1,0:T(8,128)S(1)}, u32[]{:S(2)}, u32[]{:S(2)}) %collective-permute-start) | collective-permute-done | bytes 1310752 | tf_op jit(solution)/shard_map/ppermute | solution.py:13
  42.6 163.2 %multiply_reduce_fusion = f32[40,128,20,128]{3,2,1,0:T(8,128)} fusion(f32[40,1,128,20,1,128]{5,4,3,2,1,0:T(1,128)} %param.5, f32[40,20]{1,0:T(8,128)S(1)} %select_select_fusion.3), kind=kLoop, calls=%fused_computation.8 | loop fusion | flops 13107200 | bytes 104860800 | tf_op jit(solution)/shard_map/mul | solution.py:121
  207.0 2.6 collective-permute-start.2
  209.6 52.8 %fusion.4 = f32[5120,128]{1,0:T(8,128)S(1)} fusion(f32[2560,128]{1,0:T(8,128)S(1)} %bitcast.131, f32[640,8,20,128]{3,2,1,0:T(8,128)} %bitcast.126), kind=kOutput, calls=%fused_computation.4 | convolution fusion | flops 20132659200 | bytes 56360960 | tf_op jit(solution)/shard_map/dot_general | solution.py:80
  266.8 34.0 %all-gather.1 = f32[1024,128]{1,0:T(8,128)S(1)} all-gather(f32[128,128]{1,0:T(8,128)S(1)} %convolution_bitcast_fusion.5), channel_id=3, replica_groups=mesh['row'=4,'col'=8] {'col'}, dimensions={0}, use_global_device_ids=true | all-gather | bytes 589824 | tf_op jit(solution)/shard_map/all_gather | solution.py:128
  303.2 94.1 %fusion.6 = f32[2560,128]{1,0:T(8,128)S(1)} fusion(f32[5120,128]{1,0:T(8,128)S(1)} %bitcast.137, f32[640,8,20,128]{3,2,1,0:T(8,128)} %bitcast.127), kind=kOutput, calls=%fused_computation.6 | convolution fusion | flops 20132659200 | bytes 56360960 | tf_op jit(solution)/shard_map/nm,nk->mk/dot_general | solution.py:86
  397.3 2.5 bitcast_add_fusion.1
  399.9 11.7 %cholesky.70 = f32[128,128]{1,0:T(8,128)S(1)} custom-call(f32[128,128]{1,0:T(8,128)S(1)} %fusion.25), custom_call_target="Cholesky" | custom-call | tf_op jit(solution)/shard_map/jit(cholesky)/cholesky | solution.py:43
  413.0 9.8 %custom-call.10 = f32[1,128,128]{1,2,0:T(8,128)S(1)} custom-call(f32[1,128,128]{2,1,0:T(8,128)S(1)} %fusion.15), custom_call_target="InvertDiagBlocksLowerTriangular" | custom-call | tf_op jit(solution)/shard_map/jit(_cho_solve)/triangular_solve | solution.py:44
  422.8 16.3 %all-reduce.9.cloned.1.call-done = f32[20,128,128]{2,1,0:T(8,128)} async-done(((f32[20,128,128]{2,1,0:T(8,128)}), f32[20,128,128]{2,1,0:T(8,128)}) %all-reduce.9.cloned.1.call-update) | async-done | bytes 1310736 | tf_op jit(solution)/shard_map/psum | solution.py:97
  439.1 3.5 convolution_bitcast_fusion.6
  442.6 31.7 %all-gather = f32[1024,128]{0,1:T(8,128)S(1)} all-gather(f32[128,128]{0,1:T(8,128)S(1)} %convolution_bitcast_fusion.6), channel_id=2, replica_groups=mesh['row'=4,'col'=8] {'col'}, dimensions={0}, use_global_device_ids=true | all-gather | bytes 589824 | tf_op jit(solution)/shard_map/all_gather | solution.py:128
  474.7 11.7 %cholesky.59 = f32[128,128]{1,0:T(8,128)S(1)} custom-call(f32[128,128]{1,0:T(8,128)S(1)} %fusion.31), custom_call_target="Cholesky" | custom-call | tf_op jit(solution)/shard_map/jit(cholesky)/cholesky | solution.py:43
  487.7 9.8 %custom-call.9 = f32[1,128,128]{1,2,0:T(8,128)S(1)} custom-call(f32[1,128,128]{2,1,0:T(8,128)S(1)} %fusion.14), custom_call_target="InvertDiagBlocksLowerTriangular" | custom-call | tf_op jit(solution)/shard_map/jit(_cho_solve)/triangular_solve | solution.py:44
  498.1 2.5 convolution_subtract_fusion.1
  502.8 31.3 %all-gather.2 = f32[1024,128]{1,0:T(8,128)S(1)} all-gather(f32[128,128]{1,0:T(8,128)S(1)} %convolution_bitcast_fusion.4), channel_id=4, replica_groups=mesh['row'=4,'col'=8] {'col'}, dimensions={0}, use_global_device_ids=true | all-gather | bytes 589824 | tf_op jit(solution)/shard_map/all_gather | solution.py:128
  536.9 2.8 copy.36
  543.2 17.2 %collective-permute-done.3 = f32[20,128,128]{2,1,0:T(8,128)S(1)} collective-permute-done((f32[20,128,128]{2,1,0:T(8,128)S(1)}, f32[20,128,128]{2,1,0:T(8,128)S(1)}, u32[]{:S(2)}, u32[]{:S(2)}) %collective-permute-start.3) | collective-permute-done | bytes 1310752 | tf_op jit(solution)/shard_map/ppermute | solution.py:13
  560.7 26.5 %collective-permute-done.4 = f32[20,128,128]{2,1,0:T(8,128)S(1)} collective-permute-done((f32[20,128,128]{2,1,0:T(8,128)S(1)}, f32[20,128,128]{2,1,0:T(8,128)S(1)}, u32[]{:S(2)}, u32[]{:S(2)}) %collective-permute-start.4) | collective-permute-done | bytes 1310752 | tf_op jit(solution)/shard_map/ppermute | solution.py:13
  588.9 53.3 %fusion = f32[5120,128]{1,0:T(8,128)S(1)} fusion(f32[2560,128]{1,0:T(8,128)S(1)} %bitcast.135, f32[640,8,20,128]{3,2,1,0:T(8,128)} %bitcast.128), kind=kOutput, calls=%fused_computation | convolution fusion | flops 20132659200 | bytes 56360960 | tf_op jit(solution)/shard_map/dot_general | solution.py:80
  644.0 3.0 maximum_select_fusion.1
  647.2 95.9 %fusion.2 = f32[2560,128]{1,0:T(8,128)} fusion(f32[5120,128]{1,0:T(8,128)S(1)} %bitcast.136, f32[640,8,20,128]{3,2,1,0:T(8,128)} %bitcast.129), kind=kOutput, calls=%fused_computation.2 | convolution fusion | flops 20132659200 | bytes 56360960 | tf_op jit(solution)/shard_map/nm,nk->mk/dot_general | solution.py:86
  743.1 16.5 %all-reduce.7.cloned.1.call-done = f32[20,2,128,128]{3,2,0,1:T(8,128)} async-done(((f32[20,2,128,128]{3,2,0,1:T(8,128)}), f32[20,2,128,128]{3,2,0,1:T(8,128)}) %all-reduce.7.cloned.1.call-update) | async-done | bytes 2621456 | tf_op jit(solution)/shard_map/psum | solution.py:101
  759.6 3.0 bitcast_add_fusion
  764.9 2.9 copy.33
  767.8 33.1 %all-reduce.11.cloned.1.call-done = f32[20,128,128]{2,1,0:T(8,128)} async-done(((f32[20,128,128]{2,1,0:T(8,128)}), f32[20,128,128]{2,1,0:T(8,128)}) %all-reduce.11.cloned.1.call-update) | async-done | bytes 1310736 | tf_op jit(solution)/shard_map/psum | solution.py:97
  800.9 3.5 convolution_bitcast_fusion.3
  804.4 31.5 %all-gather.3 = f32[1024,128]{1,0:T(8,128)S(1)} all-gather(f32[128,128]{1,0:T(8,128)S(1)} %convolution_bitcast_fusion.3), channel_id=5, replica_groups=mesh['row'=4,'col'=8] {'col'}, dimensions={0}, use_global_device_ids=true | all-gather | bytes 589824 | tf_op jit(solution)/shard_map/all_gather | solution.py:128
  836.0 11.7 %cholesky.81 = f32[128,128]{1,0:T(8,128)S(1)} custom-call(f32[128,128]{1,0:T(8,128)S(1)} %fusion.20), custom_call_target="Cholesky" | custom-call | tf_op jit(solution)/shard_map/jit(cholesky)/cholesky | solution.py:43
  849.1 9.8 %custom-call.11 = f32[1,128,128]{1,2,0:T(8,128)S(1)} custom-call(f32[1,128,128]{2,1,0:T(8,128)S(1)} %fusion.16), custom_call_target="InvertDiagBlocksLowerTriangular" | custom-call | tf_op jit(solution)/shard_map/jit(_cho_solve)/triangular_solve | solution.py:44
  859.4 3.7 fusion.12
  (68 shorter events, 34.0 us)
Async XLA Ops:
  7.2 390.2 %all-reduce.5.cloned.1.call-start = ((), (), s32[]{:S(2)}) async-start(), calls=%async_computation | async-start | bytes 5242880 | tf_op jit(solution)/shard_map/psum | solution.py:101
  7.2 32.0 %collective-permute-start = (f32[20,128,128]{2,1,0:T(8,128)}, f32[20,128,128]{2,1,0:T(8,128)S(1)}, u32[]{:S(2)}, u32[]{:S(2)}) collective-permute-start(f32[20,128,128]{2,1,0:T(8,128)} %bitcast.130), channel_id=1, source_target_pairs={{0,1},{1,0},{2,3},{3,2},{4,5},{5,4},{6,7},{7,6},{8,9},{9,8},{10,11... | collective-permute-start | bytes 3932168 | tf_op jit(solution)/shard_map/ppermute | solution.py:13
  40.7 165.1 %collective-permute-start.1 = (f32[20,128,128]{2,1,0:T(8,128)S(1)}, f32[20,128,128]{2,1,0:T(8,128)}, u32[]{:S(2)}, u32[]{:S(2)}) collective-permute-start(f32[20,128,128]{2,1,0:T(8,128)S(1)} %broadcast_select_fusion.1), channel_id=1, source_target_pairs={{0,2},{1,3},{2,0},{3,1},{4,6},{5,7},{6,4},{7,5},{8,10},{9,11},{10,... | collective-permute-start | bytes 3932168 | tf_op jit(solution)/shard_map/ppermute | solution.py:13
  205.8 3.8 copy-start
  207.0 93.9 %collective-permute-start.2 = (f32[20,1,128,128]{3,2,0,1:T(8,128)}, f32[20,1,128,128]{3,2,0,1:T(8,128)S(1)}, u32[]{:S(2)}, u32[]{:S(2)}) collective-permute-start(f32[20,1,128,128]{3,2,0,1:T(8,128)} %select_bitcast_fusion.1), channel_id=1, source_target_pairs={{0,4},{1,5},{2,6},{3,7},{4,0},{5,1},{6,2},{7,3},{8,12},{9,13},{10,... | collective-permute-start | bytes 3932168 | tf_op jit(solution)/shard_map/ppermute | solution.py:13
  264.2 174.9 %all-reduce.9.cloned.1.call-start = ((), (), s32[]{:S(2)}) async-start(), calls=%async_computation.2 | async-start | bytes 2621440 | tf_op jit(solution)/shard_map/psum | solution.py:97
  399.9 359.7 %all-reduce.7.cloned.1.call-start = ((), (), s32[]{:S(2)}) async-start(), calls=%async_computation.1 | async-start | bytes 5242880 | tf_op jit(solution)/shard_map/psum | solution.py:101
  541.2 47.8 %copy-start.1 = (f32[20,128,128]{2,1,0:T(8,128)}, f32[20,128,128]{2,1,0:T(8,128)S(1)}, u32[]{:S(2)}) copy-start(f32[20,128,128]{2,1,0:T(8,128)S(1)} %add.73) | copy-start | bytes 3932164
  541.2 19.2 %collective-permute-start.3 = (f32[20,128,128]{2,1,0:T(8,128)S(1)}, f32[20,128,128]{2,1,0:T(8,128)S(1)}, u32[]{:S(2)}, u32[]{:S(2)}) collective-permute-start(f32[20,128,128]{2,1,0:T(8,128)S(1)} %add.73), channel_id=1, source_target_pairs={{0,1},{1,0},{2,3},{3,2},{4,5},{5,4},{6,7},{7,6},{8,9},{9,8},{10,11... | collective-permute-start | bytes 3932168 | tf_op jit(solution)/shard_map/ppermute | solution.py:13
  560.6 26.6 %collective-permute-start.4 = (f32[20,128,128]{2,1,0:T(8,128)S(1)}, f32[20,128,128]{2,1,0:T(8,128)S(1)}, u32[]{:S(2)}, u32[]{:S(2)}) collective-permute-start(f32[20,128,128]{2,1,0:T(8,128)S(1)} %broadcast_select_fusion), channel_id=1, source_target_pairs={{0,2},{1,3},{2,0},{3,1},{4,6},{5,7},{6,4},{7,5},{8,10},{9,11},{10,... | collective-permute-start | bytes 3932168 | tf_op jit(solution)/shard_map/ppermute | solution.py:13
  588.4 55.6 %collective-permute-start.5 = (f32[20,1,128,128]{3,2,0,1:T(8,128)}, f32[20,1,128,128]{3,2,0,1:T(8,128)}, u32[]{:S(2)}, u32[]{:S(2)}) collective-permute-start(f32[20,1,128,128]{3,2,0,1:T(8,128)} %select_bitcast_fusion), channel_id=1, source_target_pairs={{0,4},{1,5},{2,6},{3,7},{4,0},{5,1},{6,2},{7,3},{8,12},{9,13},{10,... | collective-permute-start | bytes 3932168 | tf_op jit(solution)/shard_map/ppermute | solution.py:13
  643.9 157.0 %all-reduce.11.cloned.1.call-start = ((), (), s32[]{:S(2)}) async-start(), calls=%async_computation.3 | async-start | bytes 2621440 | tf_op jit(solution)/shard_map/psum | solution.py:97
  764.9 35.9 %copy-start.2 = (f32[20,128,128]{2,1,0:T(8,128)S(1)}, f32[20,128,128]{2,1,0:T(8,128)}, u32[]{:S(2)}) copy-start(f32[20,128,128]{2,1,0:T(8,128)} %copy-done.1) | copy-start | bytes 3932164
  859.4 3.7 copy-start.3
Sparse Core Ops, SparseCore 0:
  264.3 119.9 all-reduce.4
  400.0 39.0 all-reduce.8
  644.0 115.4 all-reduce.6
  762.7 38.1 all-reduce.10
